TPU v7x, 32 devices: a whole 2x2x4 slice. The times are simulated.
32 devices in a mesh: dp: 8 (over z, x), mp: 4 (over y, core).
Axes of the slice: x: 2, y: 2, z: 4, core: 2. Of those that a mesh axis runs over, the one named last changes fastest.
Arguments:
- inputs: bfloat16 [16384, 768], P('dp'), may hold values from -6 to 6
- segments: int32 [256, 64], P('dp'), may hold values from 0 to 5, never falling along the last dimension, each value on 1 to 24 neighbouring positions
- cotangent: bfloat16 [16384, 768], P('dp'), may hold values from -12 to 12
- triple_weight: float32 [3, 768, 768], P(None, 'dp', 'mp'), may hold values from -0.21875 to 0.21875
- triple_first: float32 [3, 768, 768], P(None, 'dp', 'mp')
- triple_second: float32 [3, 768, 768], P(None, 'dp', 'mp'), as said below
- outward_weight: float32 [768, 768], P('mp', 'dp'), may hold values from -0.625 to 0.625
- outward_first: float32 [768, 768], P('mp', 'dp')
- outward_second: float32 [768, 768], P('mp', 'dp'), as said below
- expand_weight: float32 [768, 3072], P('dp', 'mp'), may hold values from -2 to 2
- expand_first: float32 [768, 3072], P('dp', 'mp')
- expand_second: float32 [768, 3072], P('dp', 'mp'), as said below
- reduce_weight: float32 [3072, 768], P('mp', 'dp'), may hold values from -0.109375 to 0.109375
- reduce_first: float32 [3072, 768], P('mp', 'dp')
- reduce_second: float32 [3072, 768], P('mp', 'dp'), as said below
- norm_params: float32 [6, 768], replicated, may hold values from -3 to 4
- norm_first: float32 [6, 768], replicated
- norm_second: float32 [6, 768], replicated, as said below
- paired_bias: float32 [2, 768], P(None, 'mp'), may hold values from -1.8 to 1.8
- paired_first: float32 [2, 768], P(None, 'mp')
- paired_second: float32 [2, 768], P(None, 'mp'), as said below
- hidden_bias: float32 [3072], P('mp'), may hold values from -1.8 to 1.8
- hidden_first: float32 [3072], P('mp')
- hidden_second: float32 [3072], P('mp'), as said below
Outputs:
- outputs: bfloat16 [16384, 768], P('dp')
- input_gradient: bfloat16 [16384, 768], P('dp')
- gradient_norm: float32 [], replicated
- triple_moment: float32 [3, 768, 768], P(None, 'dp', 'mp')
- triple_square: float32 [3, 768, 768], P(None, 'dp', 'mp')
- triple_updated: float32 [3, 768, 768], P(None, 'dp', 'mp')
- outward_moment: float32 [768, 768], P('mp', 'dp')
- outward_square: float32 [768, 768], P('mp', 'dp')
- outward_updated: float32 [768, 768], P('mp', 'dp')
- expand_moment: float32 [768, 3072], P('dp', 'mp')
- expand_square: float32 [768, 3072], P('dp', 'mp')
- expand_updated: float32 [768, 3072], P('dp', 'mp')
- reduce_moment: float32 [3072, 768], P('mp', 'dp')
- reduce_square: float32 [3072, 768], P('mp', 'dp')
- reduce_updated: float32 [3072, 768], P('mp', 'dp')
- norm_moment: float32 [6, 768], replicated
- norm_square: float32 [6, 768], replicated
- norm_updated: float32 [6, 768], replicated
- paired_moment: float32 [2, 768], P(None, 'mp')
- paired_square: float32 [2, 768], P(None, 'mp')
- paired_updated: float32 [2, 768], P(None, 'mp')
- hidden_moment: float32 [3072], P('mp')
- hidden_square: float32 [3072], P('mp')
- hidden_updated: float32 [3072], P('mp')
Inputs may be any that keep to these rules, and one draw needn't show every extreme that they name: `segments`: within each row of 64 tokens the numbers never fall; each of the 6 captions holds 1 to 24 tokens, one exactly 24. `triple_second`: positive. `outward_second`: positive. `expand_second`: positive. `reduce_second`: positive. `norm_second`: positive. `paired_second`: positive. `hidden_second`: positive.
All inputs are finite; a program needn't handle non-finite values.
Results may differ from a plain program's by a relative error of at most 0.02.
Values may be sent and summed in bfloat16 or wider, within the bound.
No kernel may reach another device: no remote copies, remote signals or barrier semaphores. Data moves between devices by JAX's collectives and lax.ppermute only.
A program may use at most 128 MiB of HBM per device.

v0:
```python
import jax
import jax.numpy as jnp
from jax import lax
from jax.sharding import PartitionSpec as P

HD = 64
STEP = 5
EPS_NORM = 1e-06
BETA = 0.5
LR_MATRIX = 0.03
LR_VECTOR = 0.2
DECAY = 0.1
ADAM_EPS = 1e-08
CLIP = 1.0
NEG = -1e30


def norm_forward(rows_in, gain_row, shift_row):
    row_mean = jnp.mean(rows_in, axis=-1, keepdims=True)
    centred = rows_in - row_mean
    variance = jnp.mean(centred * centred, axis=-1, keepdims=True)
    scaled = lax.rsqrt(variance + EPS_NORM)
    normal_rows = centred * scaled
    return (normal_rows * gain_row + shift_row, normal_rows, scaled)


def norm_backward(upstream, normal_rows, scaled, gain_row):
    gained = upstream * gain_row
    mean_one = jnp.mean(gained, axis=-1, keepdims=True)
    mean_two = jnp.mean(gained * normal_rows, axis=-1, keepdims=True)
    return scaled * (gained - mean_one - normal_rows * mean_two)


def smooth_gate(values_in):
    return jax.nn.gelu(values_in, approximate=True)


def adam_step(weight, first, second, grad, factor, rate, decay):
    clipped = grad * factor
    first_new = BETA * first + (1.0 - BETA) * clipped
    second_new = BETA * second + (1.0 - BETA) * clipped * clipped
    correction = 1.0 - BETA**STEP
    direction = first_new / correction / (jnp.sqrt(second_new / correction) + ADAM_EPS)
    return (first_new, second_new, weight - rate * (direction + decay * weight))


def per_device(
    inputs,
    segments,
    cotangent,
    triple_weight,
    triple_first,
    triple_second,
    outward_weight,
    outward_first,
    outward_second,
    expand_weight,
    expand_first,
    expand_second,
    reduce_weight,
    reduce_first,
    reduce_second,
    norm_params,
    norm_first,
    norm_second,
    paired_bias,
    paired_first,
    paired_second,
    hidden_bias,
    hidden_first,
    hidden_second,
):
    f32 = jnp.float32
    bf16 = jnp.bfloat16
    dp_count = lax.axis_size("dp")
    mp_count = lax.axis_size("mp")
    triple_full, outward_full, expand_full, reduce_full = (
        lax.all_gather(triple_weight.astype(bf16), "dp", axis=1, tiled=True),
        lax.all_gather(outward_weight.astype(bf16), "dp", axis=1, tiled=True),
        lax.all_gather(expand_weight.astype(bf16), "dp", axis=0, tiled=True),
        lax.all_gather(reduce_weight.astype(bf16), "dp", axis=1, tiled=True),
    )
    row_count, row_length = segments.shape
    token_count = inputs.shape[0]
    head_width = triple_full.shape[2]
    head_count = head_width // HD
    scale_factor = HD ** (-0.5)
    grid = (row_count, row_length, head_count, HD)
    x_full = inputs.astype(f32)
    normed_one, normal_one, scaled_one = norm_forward(x_full, norm_params[0], norm_params[1])
    first_low = normed_one.astype(bf16)
    projected = jnp.einsum("td,cdw->ctw", first_low, triple_full, preferred_element_type=f32)
    queries = (projected[0] + paired_bias[0]).astype(bf16).reshape(grid)
    key_rows = projected[1].astype(bf16).reshape(grid)
    value_rows = (projected[2] + paired_bias[1]).astype(bf16).reshape(grid)
    same_caption = (segments[:, :, None] == segments[:, None, :])[:, None, :, :]

    def scores_of(query_in, key_in):
        raw_scores = jnp.einsum("rqhd,rkhd->rhqk", query_in, key_in, preferred_element_type=f32)
        return jnp.where(same_caption, raw_scores * scale_factor, NEG)

    scores = scores_of(queries, key_rows)
    row_top = jnp.max(scores, axis=-1, keepdims=True)
    lifted = jnp.exp(scores - row_top)
    row_total = jnp.sum(lifted, axis=-1, keepdims=True)
    probs = lifted / row_total
    log_total = row_top + jnp.log(row_total)
    context = jnp.einsum(
        "rhqk,rkhd->rqhd", probs.astype(bf16), value_rows, preferred_element_type=f32
    )
    context_low = context.astype(bf16).reshape(token_count, head_width)
    attn_part = jnp.dot(context_low, outward_full, preferred_element_type=f32)
    attended = lax.psum(attn_part.astype(jnp.bfloat16), "mp").astype(jnp.float32)
    middle = x_full + attended + norm_params[4]
    normed_two, normal_two, scaled_two = norm_forward(middle, norm_params[2], norm_params[3])
    second_low = normed_two.astype(bf16)
    hidden_pre = jnp.dot(second_low, expand_full, preferred_element_type=f32) + hidden_bias
    gate_out, gelu_pull = jax.vjp(smooth_gate, hidden_pre)
    activated = gate_out.astype(bf16)
    fed_part = jnp.dot(activated, reduce_full, preferred_element_type=f32)
    fed = lax.psum(fed_part.astype(jnp.bfloat16), "mp").astype(jnp.float32)
    outputs = (middle + fed + norm_params[5]).astype(bf16)
    cot_full = cotangent.astype(f32)
    grad_reduce = jnp.einsum("tf,td->fd", activated, cotangent, preferred_element_type=f32)
    act_grad = jnp.einsum("td,fd->tf", cotangent, reduce_full, preferred_element_type=f32)
    hidden_grad = gelu_pull(act_grad)[0].astype(bf16)
    grad_expand = jnp.einsum("td,tf->df", second_low, hidden_grad, preferred_element_type=f32)
    grad_hidden = jnp.sum(hidden_grad, axis=0, dtype=f32)
    second_part = jnp.einsum("tf,df->td", hidden_grad, expand_full, preferred_element_type=f32)
    second_grad = lax.psum(second_part.astype(jnp.bfloat16), "mp").astype(jnp.float32)
    middle_grad = cot_full + norm_backward(second_grad, normal_two, scaled_two, norm_params[2])
    middle_low = middle_grad.astype(bf16)
    grad_outward = jnp.einsum("tw,td->wd", context_low, middle_low, preferred_element_type=f32)
    context_grad = (
        jnp.einsum("td,wd->tw", middle_low, outward_full, preferred_element_type=f32)
        .astype(bf16)
        .reshape(grid)
    )
    probs_again = jnp.exp(scores_of(queries, key_rows) - log_total)
    probs_low = probs_again.astype(bf16)
    value_grad = jnp.einsum(
        "rhqk,rqhd->rkhd", probs_low, context_grad, preferred_element_type=f32
    ).astype(bf16)
    prob_grad = jnp.einsum("rqhd,rkhd->rhqk", context_grad, value_rows, preferred_element_type=f32)
    inner = jnp.sum(prob_grad * probs_again, axis=-1, keepdims=True)
    score_grad = (probs_again * (prob_grad - inner) * scale_factor).astype(bf16)
    query_grad = jnp.einsum(
        "rhqk,rkhd->rqhd", score_grad, key_rows, preferred_element_type=f32
    ).astype(bf16)
    key_grad = jnp.einsum(
        "rhqk,rqhd->rkhd", score_grad, queries, preferred_element_type=f32
    ).astype(bf16)
    stacked = jnp.stack([query_grad, key_grad, value_grad]).reshape(3, token_count, head_width)
    grad_triple = jnp.einsum("td,ctw->cdw", first_low, stacked, preferred_element_type=f32)
    grad_paired = jnp.stack(
        [jnp.sum(stacked[0], axis=0, dtype=f32), jnp.sum(stacked[2], axis=0, dtype=f32)]
    )
    first_part = jnp.einsum("ctw,cdw->td", stacked, triple_full, preferred_element_type=f32)
    first_grad = lax.psum(first_part.astype(jnp.bfloat16), "mp").astype(jnp.float32)
    input_gradient = (
        middle_grad + norm_backward(first_grad, normal_one, scaled_one, norm_params[0])
    ).astype(bf16)
    grad_norms = jnp.stack(
        [
            jnp.sum(first_grad * normal_one, axis=0),
            jnp.sum(first_grad, axis=0),
            jnp.sum(second_grad * normal_two, axis=0),
            jnp.sum(second_grad, axis=0),
            jnp.sum(middle_grad, axis=0),
            jnp.sum(cot_full, axis=0),
        ]
    )
    owned = (
        lax.psum_scatter(grad_triple, "dp", scatter_dimension=1, tiled=True),
        lax.psum_scatter(grad_outward, "dp", scatter_dimension=1, tiled=True),
        lax.psum_scatter(grad_expand, "dp", scatter_dimension=0, tiled=True),
        lax.psum_scatter(grad_reduce, "dp", scatter_dimension=1, tiled=True),
    )
    vectors = lax.psum((grad_norms, grad_paired, grad_hidden), "dp")
    local_square = jnp.zeros((), f32)
    for grad_item in owned:
        local_square = local_square + jnp.sum(grad_item * grad_item)
    local_square = local_square + jnp.sum(vectors[0] * vectors[0]) / (dp_count * mp_count)
    local_square = (
        local_square
        + (jnp.sum(vectors[1] * vectors[1]) + jnp.sum(vectors[2] * vectors[2])) / dp_count
    )
    total_square = lax.psum(local_square, ("dp", "mp"))
    gradient_norm = jnp.sqrt(total_square)
    factor = jnp.minimum(1.0, CLIP / gradient_norm)
    triple_new = adam_step(
        triple_weight, triple_first, triple_second, owned[0], factor, LR_MATRIX, DECAY
    )
    outward_new = adam_step(
        outward_weight, outward_first, outward_second, owned[1], factor, LR_MATRIX, DECAY
    )
    expand_new = adam_step(
        expand_weight, expand_first, expand_second, owned[2], factor, LR_MATRIX, DECAY
    )
    reduce_new = adam_step(
        reduce_weight, reduce_first, reduce_second, owned[3], factor, LR_MATRIX, DECAY
    )
    norm_new = adam_step(norm_params, norm_first, norm_second, vectors[0], factor, LR_VECTOR, 0.0)
    paired_new = adam_step(
        paired_bias, paired_first, paired_second, vectors[1], factor, LR_VECTOR, 0.0
    )
    hidden_new = adam_step(
        hidden_bias, hidden_first, hidden_second, vectors[2], factor, LR_VECTOR, 0.0
    )
    return (
        outputs,
        input_gradient,
        gradient_norm,
        triple_new[0],
        triple_new[1],
        triple_new[2],
        outward_new[0],
        outward_new[1],
        outward_new[2],
        expand_new[0],
        expand_new[1],
        expand_new[2],
        reduce_new[0],
        reduce_new[1],
        reduce_new[2],
        norm_new[0],
        norm_new[1],
        norm_new[2],
        paired_new[0],
        paired_new[1],
        paired_new[2],
        hidden_new[0],
        hidden_new[1],
        hidden_new[2],
    )


def solution(mesh):
    placed = (
        P("dp", None),
        P("dp", None),
        P("dp", None),
        P(None, "dp", "mp"),
        P(None, "dp", "mp"),
        P(None, "dp", "mp"),
        P("mp", "dp"),
        P("mp", "dp"),
        P("mp", "dp"),
        P("dp", "mp"),
        P("dp", "mp"),
        P("dp", "mp"),
        P("mp", "dp"),
        P("mp", "dp"),
        P("mp", "dp"),
        P(),
        P(),
        P(),
        P(None, "mp"),
        P(None, "mp"),
        P(None, "mp"),
        P("mp"),
        P("mp"),
        P("mp"),
    )
    return jax.shard_map(
        per_device,
        mesh=mesh,
        in_specs=placed,
        out_specs=(
            P("dp", None),
            P("dp", None),
            P(),
            P(None, "dp", "mp"),
            P(None, "dp", "mp"),
            P(None, "dp", "mp"),
            P("mp", "dp"),
            P("mp", "dp"),
            P("mp", "dp"),
            P("dp", "mp"),
            P("dp", "mp"),
            P("dp", "mp"),
            P("mp", "dp"),
            P("mp", "dp"),
            P("mp", "dp"),
            P(),
            P(),
            P(),
            P(None, "mp"),
            P(None, "mp"),
            P(None, "mp"),
            P("mp"),
            P("mp"),
            P("mp"),
        ),
        check_vma=False,
    )
```

profile of v0, /device:TPU:0, one launch (start us, length us, event | category | flops | bytes accessed | tf_op | source)
XLA Modules:
  0.0 715.4 jit_solution(5087993690982692376)
XLA Ops:
  12.8 40.5 %all_gather.12 = bf16[3,768,192]{2,0,1:T(4,128)(2,1)} all-gather(bf16[3,96,192]{2,0,1:T(4,128)(2,1)S(1)} %copy.118), channel_id=1, replica_groups=mesh['dp'=8,'mp'=4] {'dp'}, dimensions={1}, use_global_device_ids=true | all-gather | bytes 995328 | tf_op jit(solution)/shard_map/all_gather | solution.py:78
  65.1 31.9 %all_gather.13 = bf16[192,768]{0,1:T(8,128)(2,1)S(1)} all-gather(bf16[192,96]{0,1:T(8,128)(2,1)} %copy.127), channel_id=1, replica_groups=mesh['dp'=8,'mp'=4] {'dp'}, dimensions={1}, use_global_device_ids=true | all-gather | bytes 331776 | tf_op jit(solution)/shard_map/all_gather | solution.py:79
  114.9 5.7 fusion.108
  138.0 63.8 %all-reduce.6.cloned.1.call-done = bf16[2048,768]{1,0:T(8,128)(2,1)} async-done(((bf16[2048,768]{1,0:T(8,128)(2,1)}), bf16[2048,768]{1,0:T(8,128)(2,1)}) %all-reduce.6.cloned.1.call-update) | async-done | bytes 3145744 | tf_op jit(solution)/shard_map/psum | solution.py:113
  210.4 7.5 %fusion.111 = f32[2048,768]{1,0:T(8,128)} fusion(bf16[2048,768]{1,0:T(8,128)(2,1)} %add_convert_fusion.1, bf16[768,768]{1,0:T(8,128)(2,1)} %all-gather.3.cloned.1.call-done), kind=kOutput, calls=%fused_computation.161 | convolution fusion | flops 2415919104 | bytes 10616832 | tf_op jit(solution)/shard_map/dot_general | solution.py:117
  220.3 10.8 %convert_reduce_fusion.4 = (f32[768]{0:T(1024)}, bf16[2048,768]{1,0:T(8,128)(2,1)S(1)}, bf16[2048,768]{1,0:T(8,128)(2,1)}) fusion(f32[2048,768]{1,0:T(8,128)} %fusion.111, f32[768]{0:T(1024)} %param.45, bf16[2048,768]{1,0:T(8,128)(2,1)} %param.26, bf16[768,768]{0,1:T(8,128)(2,1)} %all-gather.5.cloned.1.call-done), kind=kOutput, calls=%fused_computation.46 | convolution fusion | flops 2455239936 | bytes 16914432 | tf_op jit(solution)/shard_map/td,fd->tf/dot_general | solution.py:125
  238.7 6.6 convolution_convert_fusion.1
  245.2 58.7 %all-reduce.8.cloned.1.call-done = bf16[2048,768]{1,0:T(8,128)(2,1)} async-done(((bf16[2048,768]{1,0:T(8,128)(2,1)}), bf16[2048,768]{1,0:T(8,128)(2,1)}) %all-reduce.8.cloned.1.call-update) | async-done | bytes 3145744 | tf_op jit(solution)/shard_map/psum | solution.py:130
  303.9 7.1 fusion.30
  311.1 4.7 fusion.106
  320.7 4.9 convolution_convert_fusion.3
  332.7 5.1 fusion.81
  337.8 10.3 %fusion.71 = bf16[32,64,3,64]{1,3,2,0:T(8,128)(2,1)} fusion(f32[32,3,64,64]{2,3,1,0:T(8,128)} %fusion.81, f32[32,3,64,64]{2,3,1,0:T(8,128)} %copy-done.4, f32[32,3,64]{2,1,0:T(4,128)S(1)} %copy-done.23, f32[32,64,3,64]{1,0,3,2:T(8,128)} %squeeze.10, f32[3,64]{1,0:T(4,128)S(1)} %copy-done.47), kind=kOutput, calls=%fused_computation.91 | convolution fusion | flops 54270016 | bytes 5530368 | tf_op jit(solution)/shard_map/rhqk,rqhd->rkhd/dot_general | solution.py:150
  348.1 8.1 %convert_reduce_fusion.6 = (f32[3,64]{1,0:T(4,128)S(1)}, bf16[32,64,3,64]{3,1,2,0:T(8,128)(2,1)}) fusion(bf16[32,64,3,64]{3,1,2,0:T(8,128)(2,1)} %copy.123, f32[32,3,64,64]{2,3,1,0:T(8,128)} %fusion.81, f32[32,3,64,64]{2,3,1,0:T(8,128)} %copy-done.4, f32[32,3,64]{2,1,0:T(4,128)S(1)} %copy-done.23), kind=kOutput, calls=%fused_computation.60 | convolution fusion | flops 54269824 | bytes 4743936 | tf_op jit(solution)/shard_map/rhqk,rkhd->rqhd/dot_general | solution.py:147
  387.9 6.0 bitcast_convert_fusion
  394.0 7.1 fusion.112
  401.4 6.9 fusion.113
  408.4 5.2 fusion.65
  429.0 85.0 %all-reduce.10.cloned.1.call-done = (bf16[2048,768]{1,0:T(8,128)(2,1)}, bf16[2048,768]{1,0:T(8,128)(2,1)}) async-done(((bf16[2048,768]{1,0:T(8,128)(2,1)}, bf16[2048,768]{1,0:T(8,128)(2,1)}), (bf16[2048,768]{1,0:T(8,128)(2,1)}, bf16[2048,768]{1,0:T(8,128)(2,1)})) %all-reduce.10.cloned.1.call-update) | async-done | bytes 6291472 | tf_op jit(solution)/shard_map/psum | solution.py:121
  518.7 37.3 %all-reduce = (f32[6,768]{1,0:T(8,128)S(1)}, f32[2,192]{1,0:T(2,128)S(1)}, f32[768]{0:T(1024)S(1)}) all-reduce(f32[6,768]{1,0:T(8,128)S(1)} %stack.52, f32[2,192]{1,0:T(2,128)S(1)} %pad_maximum_fusion, f32[768]{0:T(1024)S(1)} %copy-done.53), channel_id=1, replica_groups=mesh['dp'=8,'mp'=4] {'dp'}, use_global_device_ids=true, to_apply=%region_29.30 | all-reduce | flops 5760 | bytes 46080 | tf_op jit(solution)/shard_map/psum | solution.py:179
  561.4 6.3 reduce-scatter.11.cloned.1.call-done
  570.5 67.2 %reduce-scatter.13.cloned.1.call-done = f32[96,576]{1,0:T(8,128)} async-done(((f32[768,576]{1,0:T(8,128)}), f32[96,576]{1,0:T(8,128)}) %reduce-scatter.13.cloned.1.call-update) | async-done | bytes 221200
  644.0 10.6 %fusion.16 = (bf16[2048,768]{1,0:T(8,128)(2,1)}, bf16[2048,768]{1,0:T(8,128)(2,1)}) fusion(f32[2048,768]{1,0:T(8,128)} %copy-done.3, bf16[2048,768]{1,0:T(8,128)(2,1)S(1)} %copy-done, bf16[2048,768]{1,0:T(8,128)(2,1)} %get-tuple-element.140, f32[2048]{0:T(1024)} %broadcast_multiply_fusion, f32[2048]{0:T(1024)} %broadcast_multiply_fusion.1, ...), kind=kLoop, calls=%fused_computation.29 | loop fusion | flops 28311552 | bytes 25207808 | tf_op jit(solution)/shard_map/convert_element_type | solution.py:162
  654.7 39.5 %psum.63 = f32[]{:T(128)} all-reduce(f32[]{:T(128)S(6)} %add.294), channel_id=1, replica_groups=mesh['dp'=8,'mp'=4] {'dp','mp'}, use_global_device_ids=true, to_apply=%region_38.39 | all-reduce | flops 1 | bytes 8 | tf_op jit(solution)/shard_map/psum | solution.py:188
  (225 shorter events, 156.2 us)
Async XLA Ops:
  8.1 193.7 %all-reduce.6.cloned.1.call-start = ((), (), s32[]{:S(2)}) async-start(), calls=%async_computation.4 | async-start | bytes 6291456 | tf_op jit(solution)/shard_map/psum | solution.py:113
  10.9 45.8 %copy-start.25 = (f32[2048]{0:T(1024)}, f32[2048]{0:T(1024)S(1)}, u32[]{:S(2)}) copy-start(f32[2048]{0:T(1024)S(1)} %broadcast_multiply_fusion.5) | copy-start | bytes 24580
  12.0 48.1 %copy-start.32 = (f32[2048]{0:T(1024)}, f32[2048]{0:T(1024)S(1)}, u32[]{:S(2)}) copy-start(f32[2048]{0:T(1024)S(1)} %add_rsqrt_fusion.1) | copy-start | bytes 24580
  12.6 47.5 %copy-start.35 = (f32[768]{0:T(1024)}, f32[768]{0:T(1024)S(1)}, u32[]{:S(2)}) copy-start(f32[768]{0:T(1024)S(1)} %get-tuple-element.133) | copy-start | bytes 9220
  12.6 47.5 %copy-start.54 = (f32[768]{0:T(1024)}, f32[768]{0:T(1024)S(1)}, u32[]{:S(2)}) copy-start(f32[768]{0:T(1024)S(1)} %get-tuple-element.132) | copy-start | bytes 9220
  63.2 58.3 %copy-start.44 = (f32[3,64]{1,0:T(4,128)}, f32[3,64]{1,0:T(4,128)S(1)}, u32[]{:S(2)}) copy-start(f32[3,64]{1,0:T(4,128)S(1)} %add.264) | copy-start | bytes 2308
  63.3 51.6 %copy-start.46 = (f32[3,64]{1,0:T(4,128)}, f32[3,64]{1,0:T(4,128)S(1)}, u32[]{:S(2)}) copy-start(f32[3,64]{1,0:T(4,128)S(1)} %add.267) | copy-start | bytes 2308
  134.3 76.0 %all-gather.3.cloned.1.call-start = ((), (), s32[]{:S(2)}) async-start(), calls=%async_computation.5 | async-start | bytes 1327104 | tf_op jit(solution)/shard_map/all_gather | solution.py:80
  136.0 84.2 %all-gather.5.cloned.1.call-start = ((), (), s32[]{:S(2)}) async-start(), calls=%async_computation.6 | async-start | bytes 1327104 | tf_op jit(solution)/shard_map/all_gather | solution.py:81
  137.8 166.2 %all-reduce.8.cloned.1.call-start = ((), (), s32[]{:S(2)}) async-start(), calls=%async_computation.7 | async-start | bytes 6291456 | tf_op jit(solution)/shard_map/psum | solution.py:130
  236.9 190.5 %reduce-scatter.15.cloned.1.call-start = ((), (), s32[]{:S(2)}) async-start(), calls=%async_computation.11 | async-start | bytes 884736
  360.5 153.4 %all-reduce.10.cloned.1.call-start = ((), (), s32[]{:S(2)}) async-start(), calls=%async_computation.12 | async-start | bytes 12582912 | tf_op jit(solution)/shard_map/psum | solution.py:121
  394.0 165.8 %reduce-scatter.9.cloned.1.call-start = ((), (), s32[]{:S(2)}) async-start(), calls=%async_computation.8 | async-start | bytes 2654208 | tf_op jit(solution)/shard_map/reduce_scatter | solution.py:176
  401.1 166.6 %reduce-scatter.11.cloned.1.call-start = ((), (), s32[]{:S(2)}) async-start(), calls=%async_computation.9 | async-start | bytes 2654208 | tf_op jit(solution)/shard_map/reduce_scatter | solution.py:177
  408.3 229.4 %reduce-scatter.13.cloned.1.call-start = ((), (), s32[]{:S(2)}) async-start(), calls=%async_computation.10 | async-start | bytes 2211840
  556.0 83.6 %copy-start.30 = (f32[6,768]{1,0:T(8,128)}, f32[6,768]{1,0:T(8,128)S(1)}, u32[]{:S(2)}) copy-start(f32[6,768]{1,0:T(8,128)S(1)} %get-tuple-element.136) | copy-start | bytes 55300
  556.0 83.6 %copy-start.40 = (f32[768]{0:T(1024)}, f32[768]{0:T(1024)S(1)}, u32[]{:S(2)}) copy-start(f32[768]{0:T(1024)S(1)} %get-tuple-element.138) | copy-start | bytes 9220
  556.0 83.6 %copy-start.48 = (f32[2,192]{1,0:T(2,128)}, f32[2,192]{1,0:T(2,128)S(1)}, u32[]{:S(2)}) copy-start(f32[2,192]{1,0:T(2,128)S(1)} %get-tuple-element.137) | copy-start | bytes 4612
  654.7 48.5 %copy-start.18 = (f32[192,96]{1,0:T(8,128)S(1)}, f32[192,96]{1,0:T(8,128)}, u32[]{:S(2)}) copy-start(f32[192,96]{1,0:T(8,128)} %param.30) | copy-start | bytes 221188
  654.7 48.5 %copy-start.29 = (f32[192,96]{1,0:T(8,128)S(1)}, f32[192,96]{1,0:T(8,128)}, u32[]{:S(2)}) copy-start(f32[192,96]{1,0:T(8,128)} %param.32) | copy-start | bytes 221188
  654.7 50.1 %copy-start.9 = (f32[96,768]{1,0:T(8,128)S(1)}, f32[96,768]{1,0:T(8,128)}, u32[]{:S(2)}) copy-start(f32[96,768]{1,0:T(8,128)} %param.33) | copy-start | bytes 884740
  654.7 50.1 %copy-start.11 = (f32[96,768]{1,0:T(8,128)S(1)}, f32[96,768]{1,0:T(8,128)}, u32[]{:S(2)}) copy-start(f32[96,768]{1,0:T(8,128)} %reduce-scatter.9.cloned.1.call-done) | copy-start | bytes 884740
  654.7 50.1 %copy-start.19 = (f32[96,768]{1,0:T(8,128)S(1)}, f32[96,768]{1,0:T(8,128)}, u32[]{:S(2)}) copy-start(f32[96,768]{1,0:T(8,128)} %param.35) | copy-start | bytes 884740
  654.7 50.1 %copy-start.20 = (f32[96,768]{1,0:T(8,128)S(1)}, f32[96,768]{1,0:T(8,128)}, u32[]{:S(2)}) copy-start(f32[96,768]{1,0:T(8,128)} %param.34) | copy-start | bytes 884740
  (43 other events, 390.6 us)
Sparse Core Ops, SparseCore 0:
  134.4 67.2 all-reduce.5
  237.0 66.9 all-reduce.7
  394.1 119.8 all-reduce.9
Sparse Core Ops, SparseCore 1:
  137.6 40.2 all-gather.2
  180.5 39.8 all-gather.4
  360.6 62.6 reduce-scatter.14
  427.2 68.3 reduce-scatter.8
  499.5 68.2 reduce-scatter.10
  571.6 66.1 reduce-scatter.12
where the time goes:
time: 722 us; the launch traced here: 715 us
  waiting for transfers between devices  284 us (39%)
  blocking collectives  149 us (21%)
  matrix products  103 us (14%)
  local copies, waits for them, and re-layouts  94 us (13%)
  other arithmetic  62.2 us (9%)
  between operations  22.6 us (3%)
    psum x1, waiting for transfers between devices, per_device(): fed = lax.psum(fed_part.astype(jnp.bfloat16), 'mp').astype(jnp.float32)  85 us
    unnamed x11, waiting for transfers between devices  67.4 us
    psum x1, waiting for transfers between devices, per_device(): lax.psum(attn_part.astype(jnp.bfloat16), 'mp').astype(jnp.float32)  63.8 us
    psum x1, waiting for transfers between devices, per_device(): lax.psum(second_part.astype(jnp.bfloat16), 'mp').astype(jnp.float32)  58.7 us
    all_gather x1, blocking collectives, per_device(): lax.all_gather(triple_weight.astype(bf16), 'dp', axis=1, tiled=True)  40.5 us
    psum x1, blocking collectives, per_device(): total_square = lax.psum(local_square, ('dp', 'mp'))  39.5 us
    psum x1, blocking collectives, per_device(): vectors = lax.psum((grad_norms, grad_paired, grad_hidden), 'dp')  37.3 us
    unnamed x130, local copies, waits for them, and re-layouts  32.6 us
  transfers between devices with their start and end apart: 9, of which 6 were waited for; matrix products, arithmetic and copies ran while one was open for 15% of the time, Pallas kernels for 0%

commit v1 on v0

--- a/solution.py
+++ b/solution.py
@@ -118,7 +118,7 @@
     gate_out, gelu_pull = jax.vjp(smooth_gate, hidden_pre)
     activated = gate_out.astype(bf16)
     fed_part = jnp.dot(activated, reduce_full, preferred_element_type=f32)
-    fed = lax.psum(fed_part.astype(jnp.bfloat16), "mp").astype(jnp.float32)
+    fed = jnp.sum(lax.all_gather(fed_part.astype(jnp.bfloat16), "mp"), axis=0).astype(jnp.float32)
     outputs = (middle + fed + norm_params[5]).astype(bf16)
     cot_full = cotangent.astype(f32)
     grad_reduce = jnp.einsum("tf,td->fd", activated, cotangent, preferred_element_type=f32)

time: 722 us -> 677 us (0.938)
  waiting for transfers between devices: 284 us -> 232 us
  other arithmetic: 62.2 us -> 71 us
    all_gather x0 -> x1, waiting for transfers between devices: none -> 76.9 us  [per_device(): lax.all_gather(fed_part.astype(jnp.bfloat16), 'mp')]
    unnamed x11 -> x12, waiting for transfers between devices: 67.4 us -> 13 us
    psum x1, waiting for transfers between devices: 85 us -> 31.1 us  [per_device(): lax.psum(first_part.astype(jnp.bfloat16), 'mp').astype(jnp.float32)]
    psum x1, waiting for transfers between devices: 58.7 us -> 44.7 us  [per_device(): lax.psum(second_part.astype(jnp.bfloat16), 'mp').astype(jnp.float32)]
    reduce_sum x0 -> x1, other arithmetic: none -> 9.01 us  [per_device(): jnp.sum(lax.all_gather(fed_part.astype(jnp.bfloat16), 'mp'), axis=0)]
    unnamed x130 -> x122, local copies, waits for them, and re-layouts: 32.6 us -> 33.4 us
  transfers between devices with their start and end apart: 9 -> 10, of which waited for: 6 -> 6; matrix products, arithmetic and copies ran while one was open for 15% -> 26% of each run, Pallas kernels for 0% -> 0%
where the time goes in v1:
time: 677 us; the launch traced here: 670 us
  waiting for transfers between devices  232 us (34%)
  blocking collectives  147 us (22%)
  matrix products  102 us (15%)
  local copies, waits for them, and re-layouts  94.6 us (14%)
  other arithmetic  71 us (10%)
  between operations  22.4 us (3%)
    all_gather x1, waiting for transfers between devices, per_device(): lax.all_gather(fed_part.astype(jnp.bfloat16), 'mp')  76.9 us
    psum x1, waiting for transfers between devices, per_device(): lax.psum(attn_part.astype(jnp.bfloat16), 'mp').astype(jnp.float32)  63.4 us
    psum x1, waiting for transfers between devices, per_device(): lax.psum(second_part.astype(jnp.bfloat16), 'mp').astype(jnp.float32)  44.7 us
    all_gather x1, blocking collectives, per_device(): lax.all_gather(triple_weight.astype(bf16), 'dp', axis=1, tiled=True)  40.5 us
    psum x1, blocking collectives, per_device(): vectors = lax.psum((grad_norms, grad_paired, grad_hidden), 'dp')  37.6 us
    psum x1, blocking collectives, per_device(): total_square = lax.psum(local_square, ('dp', 'mp'))  36.9 us
    unnamed x122, local copies, waits for them, and re-layouts  33.4 us
    all_gather x1, blocking collectives, per_device(): lax.all_gather(outward_weight.astype(bf16), 'dp', axis=1, tiled=True)  31.8 us
  transfers between devices with their start and end apart: 10, of which 6 were waited for; matrix products, arithmetic and copies ran while one was open for 26% of the time, Pallas kernels for 0%

profile of v1, /device:TPU:0, one launch (start us, length us, event | category | flops | bytes accessed | tf_op | source)
XLA Modules:
  0.0 670.2 jit_solution(7695421517334138171)
XLA Ops:
  12.8 40.5 %all_gather.18 = bf16[3,768,192]{2,0,1:T(4,128)(2,1)} all-gather(bf16[3,96,192]{2,0,1:T(4,128)(2,1)S(1)} %copy.118), channel_id=1, replica_groups=mesh['dp'=8,'mp'=4] {'dp'}, dimensions={1}, use_global_device_ids=true | all-gather | bytes 995328 | tf_op jit(solution)/shard_map/all_gather | solution.py:78
  65.1 31.8 %all_gather.19 = bf16[192,768]{0,1:T(8,128)(2,1)S(1)} all-gather(bf16[192,96]{0,1:T(8,128)(2,1)} %copy.127), channel_id=1, replica_groups=mesh['dp'=8,'mp'=4] {'dp'}, dimensions={1}, use_global_device_ids=true | all-gather | bytes 331776 | tf_op jit(solution)/shard_map/all_gather | solution.py:79
  114.7 5.7 fusion.108
  138.2 63.4 %all-reduce.5.cloned.1.call-done = bf16[2048,768]{1,0:T(8,128)(2,1)} async-done(((bf16[2048,768]{1,0:T(8,128)(2,1)}), bf16[2048,768]{1,0:T(8,128)(2,1)}) %all-reduce.5.cloned.1.call-update) | async-done | bytes 3145744 | tf_op jit(solution)/shard_map/psum | solution.py:113
  210.1 7.5 %fusion.111 = f32[2048,768]{1,0:T(8,128)} fusion(bf16[2048,768]{1,0:T(8,128)(2,1)} %add_convert_fusion.1, bf16[768,768]{1,0:T(8,128)(2,1)} %all-gather.5.cloned.1.call-done), kind=kOutput, calls=%fused_computation.161 | convolution fusion | flops 2415919104 | bytes 10616832 | tf_op jit(solution)/shard_map/dot_general | solution.py:117
  220.1 10.8 %convert_reduce_fusion.4 = (f32[768]{0:T(1024)}, bf16[2048,768]{1,0:T(8,128)(2,1)S(1)}, bf16[2048,768]{1,0:T(8,128)(2,1)}) fusion(f32[2048,768]{1,0:T(8,128)} %fusion.111, f32[768]{0:T(1024)} %param.45, bf16[2048,768]{1,0:T(8,128)(2,1)} %param.26, bf16[768,768]{0,1:T(8,128)(2,1)} %all-gather.7.cloned.1.call-done), kind=kOutput, calls=%fused_computation.46 | convolution fusion | flops 2455239936 | bytes 16914432 | tf_op jit(solution)/shard_map/td,fd->tf/dot_general | solution.py:125
  236.7 6.5 convolution_convert_fusion.1
  243.5 6.9 %fusion.112 = f32[768,768]{1,0:T(8,128)} fusion(bf16[2048,768]{1,0:T(8,128)(2,1)} %add_convert_fusion.1, bf16[2048,768]{1,0:T(8,128)(2,1)} %copy-done.53), kind=kOutput, calls=%fused_computation.162 | convolution fusion | flops 2415919104 | bytes 8650752 | tf_op jit(solution)/shard_map/td,tf->df/dot_general | solution.py:127
  250.5 6.9 %fusion.113 = f32[768,768]{0,1:T(8,128)} fusion(bf16[2048,768]{1,0:T(8,128)(2,1)} %get-tuple-element.165, bf16[2048,768]{1,0:T(8,128)(2,1)} %param.26), kind=kOutput, calls=%fused_computation.163 | convolution fusion | flops 2415919104 | bytes 8650752 | tf_op jit(solution)/shard_map/tf,td->fd/dot_general | solution.py:124
  259.0 44.7 %all-reduce.7.cloned.1.call-done = bf16[2048,768]{1,0:T(8,128)(2,1)} async-done(((bf16[2048,768]{1,0:T(8,128)(2,1)}), bf16[2048,768]{1,0:T(8,128)(2,1)}) %all-reduce.7.cloned.1.call-update) | async-done | bytes 3145744 | tf_op jit(solution)/shard_map/psum | solution.py:130
  303.8 6.3 fusion.30
  310.7 76.9 %all-gather.9.cloned.1.call-done = bf16[8192,768]{1,0:T(8,128)(2,1)} async-done(((bf16[2048,768]{1,0:T(8,128)(2,1)}), bf16[8192,768]{1,0:T(8,128)(2,1)}) %all-gather.9.cloned.1.call-update) | async-done | bytes 12582928 | tf_op jit(solution)/shard_map/all_gather | solution.py:121
  387.6 9.0 %reduce_sum.251 = bf16[2048,768]{1,0:T(8,128)(2,1)} reduce(bf16[4,2048,768]{2,1,0:T(8,128)(2,1)} %bitcast.78, bf16[]{:T(256)} %constant.36.clone.1), dimensions={0}, to_apply=%region_7.8 | reduce | flops 4718592 | bytes 15728642 | tf_op jit(solution)/shard_map/reduce_sum | solution.py:121
  396.6 9.3 %fusion.106 = (f32[768]{0:T(1024)}, f32[2048,768]{1,0:T(8,128)S(1)}, bf16[2048,768]{1,0:T(8,128)(2,1)}, f32[768]{0:T(1024)}) fusion(f32[2048]{0:T(1024)} %get-tuple-element.175, f32[2048]{0:T(1024)S(1)} %broadcast_multiply_fusion.4, f32[768]{0:T(1024)S(1)} %get-tuple-element.131, bf16[2048,768]{1,0:T(8,128)(2,1)} %all-reduce.5.cloned.1.call-done, ...), kind=kLoop, calls=%fused_computation.158 | loop fusion | flops 31455744 | bytes 25213952 | tf_op jit(solution)/shard_map/reduce_sum | solution.py:169
  422.6 8.0 %convert_reduce_fusion.6 = (f32[3,64]{1,0:T(4,128)S(1)}, bf16[32,64,3,64]{3,1,2,0:T(8,128)(2,1)}) fusion(bf16[32,64,3,64]{3,1,2,0:T(8,128)(2,1)} %copy.123, f32[32,3,64,64]{2,3,1,0:T(8,128)} %fusion.81, f32[32,3,64,64]{2,3,1,0:T(8,128)} %copy-done.3, f32[32,3,64]{2,1,0:T(4,128)S(1)} %copy-done.20), kind=kOutput, calls=%fused_computation.60 | convolution fusion | flops 54269824 | bytes 4743936 | tf_op jit(solution)/shard_map/rhqk,rkhd->rqhd/dot_general | solution.py:147
  437.5 10.1 %fusion.71 = bf16[32,64,3,64]{1,3,2,0:T(8,128)(2,1)} fusion(f32[32,3,64,64]{2,3,1,0:T(8,128)} %fusion.81, f32[32,3,64,64]{2,3,1,0:T(8,128)} %copy-done.3, f32[32,3,64]{2,1,0:T(4,128)S(1)} %copy-done.20, f32[32,64,3,64]{1,0,3,2:T(8,128)} %squeeze.10, f32[3,64]{1,0:T(4,128)S(1)} %copy-done.41), kind=kOutput, calls=%fused_computation.91 | convolution fusion | flops 54270016 | bytes 5530368 | tf_op jit(solution)/shard_map/rhqk,rqhd->rkhd/dot_general | solution.py:150
  451.9 5.1 fusion.78
  477.7 6.0 bitcast_convert_fusion
  484.4 5.2 fusion.65
  506.7 12.8 %reduce-scatter.15.cloned.1.call-done = f32[96,192]{1,0:T(8,128)} async-done(((f32[768,192]{1,0:T(8,128)}), f32[96,192]{1,0:T(8,128)}) %reduce-scatter.15.cloned.1.call-update) | async-done | bytes 73744
  521.2 31.1 %all-reduce.9.cloned.1.call-done = bf16[2048,768]{1,0:T(8,128)(2,1)} async-done(((bf16[2048,768]{1,0:T(8,128)(2,1)}), bf16[2048,768]{1,0:T(8,128)(2,1)}) %all-reduce.9.cloned.1.call-update) | async-done | bytes 3145744 | tf_op jit(solution)/shard_map/psum | solution.py:159
  557.0 37.6 %all-reduce = (f32[6,768]{1,0:T(8,128)S(1)}, f32[2,192]{1,0:T(2,128)S(1)}, f32[768]{0:T(1024)S(1)}) all-reduce(f32[6,768]{1,0:T(8,128)S(1)} %stack.52, f32[2,192]{1,0:T(2,128)S(1)} %pad_maximum_fusion, f32[768]{0:T(1024)S(1)} %copy-done.49), channel_id=1, replica_groups=mesh['dp'=8,'mp'=4] {'dp'}, use_global_device_ids=true, to_apply=%region_29.30 | all-reduce | flops 5760 | bytes 46080 | tf_op jit(solution)/shard_map/psum | solution.py:179
  605.9 6.1 fusion.16
  612.1 36.9 %psum.55 = f32[]{:T(128)} all-reduce(f32[]{:T(128)S(6)} %add.292), channel_id=1, replica_groups=mesh['dp'=8,'mp'=4] {'dp','mp'}, use_global_device_ids=true, to_apply=%region_38.39 | all-reduce | flops 1 | bytes 8 | tf_op jit(solution)/shard_map/psum | solution.py:188
  (221 shorter events, 162.5 us)
Async XLA Ops:
  8.1 193.5 %all-reduce.5.cloned.1.call-start = ((), (), s32[]{:S(2)}) async-start(), calls=%async_computation.4 | async-start | bytes 6291456 | tf_op jit(solution)/shard_map/psum | solution.py:113
  10.9 45.8 %copy-start.22 = (f32[2048]{0:T(1024)}, f32[2048]{0:T(1024)S(1)}, u32[]{:S(2)}) copy-start(f32[2048]{0:T(1024)S(1)} %broadcast_multiply_fusion.5) | copy-start | bytes 24580
  12.0 48.1 %copy-start.28 = (f32[2048]{0:T(1024)}, f32[2048]{0:T(1024)S(1)}, u32[]{:S(2)}) copy-start(f32[2048]{0:T(1024)S(1)} %add_rsqrt_fusion.1) | copy-start | bytes 24580
  12.6 47.5 %copy-start.31 = (f32[768]{0:T(1024)}, f32[768]{0:T(1024)S(1)}, u32[]{:S(2)}) copy-start(f32[768]{0:T(1024)S(1)} %get-tuple-element.133) | copy-start | bytes 9220
  12.6 47.5 %copy-start.50 = (f32[768]{0:T(1024)}, f32[768]{0:T(1024)S(1)}, u32[]{:S(2)}) copy-start(f32[768]{0:T(1024)S(1)} %get-tuple-element.132) | copy-start | bytes 9220
  63.2 58.1 %copy-start.42 = (f32[3,64]{1,0:T(4,128)}, f32[3,64]{1,0:T(4,128)S(1)}, u32[]{:S(2)}) copy-start(f32[3,64]{1,0:T(4,128)S(1)} %add.262) | copy-start | bytes 2308
  63.3 51.4 %copy-start.40 = (f32[3,64]{1,0:T(4,128)}, f32[3,64]{1,0:T(4,128)S(1)}, u32[]{:S(2)}) copy-start(f32[3,64]{1,0:T(4,128)S(1)} %add.265) | copy-start | bytes 2308
  134.1 76.0 %all-gather.5.cloned.1.call-start = ((), (), s32[]{:S(2)}) async-start(), calls=%async_computation.5 | async-start | bytes 1327104 | tf_op jit(solution)/shard_map/all_gather | solution.py:80
  135.8 84.3 %all-gather.7.cloned.1.call-start = ((), (), s32[]{:S(2)}) async-start(), calls=%async_computation.6 | async-start | bytes 1327104 | tf_op jit(solution)/shard_map/all_gather | solution.py:81
  137.5 166.2 %all-reduce.7.cloned.1.call-start = ((), (), s32[]{:S(2)}) async-start(), calls=%async_computation.7 | async-start | bytes 6291456 | tf_op jit(solution)/shard_map/psum | solution.py:130
  236.7 150.9 %all-gather.9.cloned.1.call-start = ((), (), s32[]{:S(2)}) async-start(), calls=%async_computation.11 | async-start | bytes 15728640 | tf_op jit(solution)/shard_map/all_gather | solution.py:121
  243.3 260.0 %reduce-scatter.9.cloned.1.call-start = ((), (), s32[]{:S(2)}) async-start(), calls=%async_computation.9 | async-start | bytes 2654208 | tf_op jit(solution)/shard_map/reduce_scatter | solution.py:176
  250.4 254.4 %reduce-scatter.11.cloned.1.call-start = ((), (), s32[]{:S(2)}) async-start(), calls=%async_computation.10 | async-start | bytes 2654208 | tf_op jit(solution)/shard_map/reduce_scatter | solution.py:177
  257.5 262.1 %reduce-scatter.15.cloned.1.call-start = ((), (), s32[]{:S(2)}) async-start(), calls=%async_computation.13 | async-start | bytes 884736
  457.0 95.3 %all-reduce.9.cloned.1.call-start = ((), (), s32[]{:S(2)}) async-start(), calls=%async_computation.8 | async-start | bytes 6291456 | tf_op jit(solution)/shard_map/psum | solution.py:159
  483.7 115.8 %reduce-scatter.13.cloned.1.call-start = ((), (), s32[]{:S(2)}) async-start(), calls=%async_computation.12 | async-start | bytes 2211840
  612.0 43.2 %copy-start.39 = (f32[768]{0:T(1024)S(1)}, f32[768]{0:T(1024)}, u32[]{:S(2)}) copy-start(f32[768]{0:T(1024)} %copy-done.38) | copy-start | bytes 9220
  612.0 43.1 %copy-start.48 = (f32[768]{0:T(1024)S(1)}, f32[768]{0:T(1024)}, u32[]{:S(2)}) copy-start(f32[768]{0:T(1024)} %param.45) | copy-start | bytes 9220
  612.0 45.9 %copy-start.15 = (f32[192,96]{1,0:T(8,128)S(1)}, f32[192,96]{1,0:T(8,128)}, u32[]{:S(2)}) copy-start(f32[192,96]{1,0:T(8,128)} %param.30) | copy-start | bytes 221188
  612.0 45.9 %copy-start.25 = (f32[192,96]{1,0:T(8,128)S(1)}, f32[192,96]{1,0:T(8,128)}, u32[]{:S(2)}) copy-start(f32[192,96]{1,0:T(8,128)} %param.32) | copy-start | bytes 221188
  612.0 47.5 %copy-start.6 = (f32[96,768]{1,0:T(8,128)S(1)}, f32[96,768]{1,0:T(8,128)}, u32[]{:S(2)}) copy-start(f32[96,768]{1,0:T(8,128)} %param.33) | copy-start | bytes 884740
  612.1 47.5 %copy-start.8 = (f32[96,768]{1,0:T(8,128)S(1)}, f32[96,768]{1,0:T(8,128)}, u32[]{:S(2)}) copy-start(f32[96,768]{1,0:T(8,128)} %reduce-scatter.9.cloned.1.call-done) | copy-start | bytes 884740
  612.1 47.5 %copy-start.16 = (f32[96,768]{1,0:T(8,128)S(1)}, f32[96,768]{1,0:T(8,128)}, u32[]{:S(2)}) copy-start(f32[96,768]{1,0:T(8,128)} %param.35) | copy-start | bytes 884740
  612.1 47.5 %copy-start.17 = (f32[96,768]{1,0:T(8,128)S(1)}, f32[96,768]{1,0:T(8,128)}, u32[]{:S(2)}) copy-start(f32[96,768]{1,0:T(8,128)} %param.34) | copy-start | bytes 884740
  (40 other events, 296.2 us)
Sparse Core Ops, SparseCore 0:
  134.2 67.3 all-reduce.4
  236.8 66.9 all-reduce.6
  305.3 82.2 all-gather.8
  483.8 68.4 all-reduce.8
Sparse Core Ops, SparseCore 1:
  137.3 40.2 all-gather.4
  180.2 39.8 all-gather.6
  250.5 67.7 reduce-scatter.8
  321.8 68.1 reduce-scatter.10
  457.1 62.4 reduce-scatter.14
  523.5 66.5 reduce-scatter.12
